TPU v7x, 32 devices: a whole 2x2x4 slice. The times are simulated.
32 devices in a mesh: groups: 2 (over y), tiles: 4 (over z), rhs: 2 (over x), sub: 2 (over core).
Axes of the slice: x: 2, y: 2, z: 4, core: 2. Of those that a mesh axis runs over, the one named last changes fastest.
Arguments:
- sources: bfloat16 [256, 8192], P('rhs', ('groups', 'tiles', 'sub')), parts along dimension 1, may hold values from -6 to 6
- basis_out: bfloat16 [384, 64, 512], P(('groups', 'tiles', 'rhs', 'sub')), parts along dimension 0, may hold values from -0.15625 to 0.15625
- basis_in: bfloat16 [384, 64, 512], P(('groups', 'tiles', 'rhs', 'sub')), parts along dimension 0, may hold values from -0.25 to 0.25
- tile_rank: int32 [384], P(('groups', 'tiles', 'rhs', 'sub')), parts along dimension 0, may hold values from 1 to 64, as said below
- tile_row: int32 [384], P(('groups', 'tiles', 'rhs', 'sub')), parts along dimension 0, may hold values from 0 to 7
- tile_col: int32 [384], P(('groups', 'tiles', 'rhs', 'sub')), parts along dimension 0, may hold values from 0 to 7
- near_blocks: bfloat16 [16, 16, 512, 512], P(('groups', 'tiles', 'sub')), parts along dimension 0, may hold values from -0.0625 to 0.0625
- near_col: int32 [16, 16], P(('groups', 'tiles', 'sub')), parts along dimension 0, may hold values from 0 to 7
- jacobi_inverse: bfloat16 [64, 128, 128], P(('groups', 'tiles', 'sub')), parts along dimension 0
Outputs:
- first_result: bfloat16 [256, 8192], P('rhs', ('groups', 'tiles', 'sub')), parts along dimension 1
- second_result: bfloat16 [256, 8192], P('rhs', ('groups', 'tiles', 'sub')), parts along dimension 1
There are 2 independent parts, one for each index of `groups`. A program takes and returns all parts, laid end to end along the dimension named above; each array names one. Nothing has to cross between parts.
Inputs may be any that keep to these rules, and one draw needn't show every extreme that they name: `tile_rank`: every rank lies in 1 to 64, and some tile has rank 64.
All inputs are finite; a program needn't handle non-finite values.
Results may differ from a plain program's by a relative error of at most 0.03.
Values may be sent and summed in bfloat16 or wider, within the bound.
No kernel may reach another device: no remote copies, remote signals or barrier semaphores. Data moves between devices by JAX's collectives and lax.ppermute only.
A program may use at most 128 MiB of HBM per device.

v0:
```python
import jax
import jax.numpy as jnp
from jax import lax
from jax.sharding import PartitionSpec as P

BLK = 512
RMAX = 64
JB = 128


def tile_terms(running, pieces, gathered):
    basis_out, basis_in, tile_rank, tile_row, tile_col = pieces
    picked = jnp.take(gathered, tile_col, axis=1)
    coefficients = jnp.einsum("ctq,trq->ctr", picked, basis_in, preferred_element_type=jnp.float32)
    rank_iota = lax.broadcasted_iota(jnp.int32, (1, tile_rank.shape[0], RMAX), 2)
    kept_mask = rank_iota < tile_rank[None, :, None]
    coefficients = jnp.where(kept_mask, coefficients, jnp.zeros_like(coefficients)).astype(
        jnp.bfloat16
    )
    contrib = jnp.einsum(
        "ctr,trp->ctp", coefficients, basis_out, preferred_element_type=jnp.float32
    )
    upper = contrib.astype(jnp.bfloat16)
    lower = (contrib - upper.astype(jnp.float32)).astype(jnp.bfloat16)
    block_iota = lax.broadcasted_iota(jnp.int32, (1, running.shape[1]), 1)
    onehot = (tile_row[:, None] == block_iota).astype(jnp.bfloat16)
    placed_upper = jnp.einsum("ctp,tb->cbp", upper, onehot, preferred_element_type=jnp.float32)
    placed_lower = jnp.einsum("ctp,tb->cbp", lower, onehot, preferred_element_type=jnp.float32)
    return placed_upper + placed_lower


def apply_operator(vector, tile_apply, near_blocks, near_col):
    columns = vector.shape[0]
    gathered = lax.all_gather(vector, ("tiles", "sub"), axis=1, tiled=True).reshape(
        columns, -1, BLK
    )
    zero_sums = jnp.zeros(gathered.shape, jnp.float32)
    far_field = tile_apply(zero_sums, gathered).reshape(columns, -1)
    far_field = lax.psum_scatter(
        far_field.astype(jnp.bfloat16), ("tiles", "sub"), scatter_dimension=1, tiled=True
    ).astype(jnp.float32)
    picked = jnp.take(gathered, near_col, axis=1)
    near_field = jnp.einsum(
        "cikq,ikpq->cip", picked, near_blocks, preferred_element_type=jnp.float32
    )
    return (far_field + near_field.reshape(columns, -1)).astype(jnp.bfloat16)


def precondition(field, jacobi_inverse):
    columns = field.shape[0]
    grouped = field.reshape(columns, -1, JB)
    result = jnp.einsum("cgq,gpq->cgp", grouped, jacobi_inverse, preferred_element_type=jnp.float32)
    return result.astype(jnp.bfloat16).reshape(columns, -1)


def local(
    sources,
    basis_out,
    basis_in,
    tile_rank,
    tile_row,
    tile_col,
    near_blocks,
    near_col,
    jacobi_inverse,
):

    def tile_apply(running, gathered):
        return tile_terms(
            running,
            (
                lax.all_gather(basis_out, "rhs", axis=0, tiled=True),
                lax.all_gather(basis_in, "rhs", axis=0, tiled=True),
                lax.all_gather(tile_rank, "rhs", axis=0, tiled=True),
                lax.all_gather(tile_row, "rhs", axis=0, tiled=True),
                lax.all_gather(tile_col, "rhs", axis=0, tiled=True),
            ),
            gathered,
        )

    first_result = precondition(
        apply_operator(sources, tile_apply, near_blocks, near_col), jacobi_inverse
    )
    second_result = precondition(
        apply_operator(first_result, tile_apply, near_blocks, near_col), jacobi_inverse
    )
    return (first_result, second_result)


def solution(mesh):
    return jax.shard_map(
        local,
        mesh=mesh,
        in_specs=(
            P("rhs", ("groups", "tiles", "sub")),
            P(("groups", "tiles", "rhs", "sub"), None, None),
            P(("groups", "tiles", "rhs", "sub"), None, None),
            P(("groups", "tiles", "rhs", "sub")),
            P(("groups", "tiles", "rhs", "sub")),
            P(("groups", "tiles", "rhs", "sub")),
            P(("groups", "tiles", "sub"), None, None, None),
            P(("groups", "tiles", "sub"), None),
            P(("groups", "tiles", "sub"), None, None),
        ),
        out_specs=(P("rhs", ("groups", "tiles", "sub")), P("rhs", ("groups", "tiles", "sub"))),
        check_vma=False,
    )
```

profile of v0, /device:TPU:0, one launch (start us, length us, event | category | flops | bytes accessed | tf_op | source)
XLA Modules:
  0.0 233.3 jit_solution(618950563438700425)
XLA Ops:
  7.2 1.7 copy.40
  10.5 1.2 dynamic-slice
  14.9 5.2 %all-reduce.3 = (s32[24]{0:T(128)S(1)}, s32[24]{0:T(128)S(1)}, s32[24]{0:T(128)S(1)}) all-reduce(s32[24]{0:T(128)S(1)} %dynamic-update-slice.2, s32[24]{0:T(128)S(1)} %dynamic-update-slice.1, s32[24]{0:T(128)S(1)} %dynamic-update-slice), channel_id=1, replica_groups=mesh['groups'=2,'tiles'=4,'rhs'=2,'sub'=2] {'rhs'}, use_global_device_ids=true, to_apply=%add.2 | all-reduce | flops 72 | bytes 576
  20.2 14.8 %all-gather.5.cloned.1.call-done = bf16[128,4096]{0,1:T(8,128)(2,1)} async-done(((bf16[128,512]{0,1:T(8,128)(2,1)}), bf16[128,4096]{0,1:T(8,128)(2,1)}) %all-gather.5.cloned.1.call-update) | async-done | bytes 1048592 | tf_op jit(solution)/shard_map/all_gather | solution.py:34
  35.0 1.5 copy.41
  36.5 2.5 %gather_fusion = bf16[24,128,512]{2,1,0:T(8,128)(2,1)} fusion(bf16[128,8,512]{2,0,1:T(8,128)(2,1)S(1)} %copy.41, s32[1024]{0:T(1024)S(1)} %pad_clamp_fusion.1), kind=kCustom, calls=%fused_computation.clone | custom fusion | bytes 6291552 | tf_op jit(solution)/shard_map/jit(_take)/gather | solution.py:13
  39.0 24.4 %all-gather.7.cloned.1.call-done = bf16[24,64,512]{2,1,0:T(8,128)(2,1)} async-done(((bf16[12,64,512]{2,1,0:T(8,128)(2,1)}), bf16[24,64,512]{2,1,0:T(8,128)(2,1)}) %all-gather.7.cloned.1.call-update) | async-done | bytes 1572880 | tf_op jit(solution)/shard_map/all_gather | solution.py:73
  63.4 28.8 %all-gather.9.cloned.1.call-done = bf16[24,64,512]{2,1,0:T(8,128)(2,1)} async-done(((bf16[12,64,512]{2,1,0:T(8,128)(2,1)}), bf16[24,64,512]{2,1,0:T(8,128)(2,1)}) %all-gather.9.cloned.1.call-update) | async-done | bytes 1572880 | tf_op jit(solution)/shard_map/all_gather | solution.py:72
  92.2 7.7 %fusion.5 = (bf16[128,24,512]{2,0,1:T(8,128)(2,1)}, bf16[128,24,512]{2,0,1:T(8,128)(2,1)}) fusion(bf16[24,64,512]{2,1,0:T(8,128)(2,1)} %all-gather.9.cloned.1.call-done, bf16[24,64,512]{2,1,0:T(8,128)(2,1)} %all-gather.7.cloned.1.call-done, bf16[24,128,512]{2,1,0:T(8,128)(2,1)} %gather_fusion, pred[24]{0:T(512)(128)(4,1)S(1)} %compare_and_fusion, ...), kind=kOutput, calls=%fused_computation.13 | convolution fusion | flops 410910720 | bytes 12584472 | tf_op jit(solution)/shard_map/ctr,trp->ctp/dot_general | solution.py:20
  100.0 4.3 %fusion.14 = f32[8,128,512]{2,0,1:T(8,128)S(1)} fusion(bf16[128,24,512]{2,0,1:T(8,128)(2,1)} %get-tuple-element.17, s32[24]{0:T(128)S(1)} %get-tuple-element.14), kind=kOutput, calls=%fused_computation.22 | convolution fusion | flops 25166016 | bytes 5242976 | tf_op jit(solution)/shard_map/ctp,tb->cbp/dot_general | solution.py:28
  104.2 2.3 add_convert_fusion.1
  106.5 1.4 copy.56
  108.7 31.8 %reduce-scatter.3.cloned.1.call-done = bf16[128,512]{1,0:T(8,128)(2,1)} async-done(((bf16[128,4096]{1,0:T(8,128)(2,1)}), bf16[128,512]{1,0:T(8,128)(2,1)}) %reduce-scatter.3.cloned.1.call-update) | async-done | bytes 131088 | tf_op jit(solution)/shard_map/reduce_scatter | solution.py:39
  140.6 6.2 %fusion.93 = bf16[16,4,8,128]{3,2,1,0:T(8,128)(2,1)S(1)} fusion(bf16[1,16,512,512]{3,2,1,0:T(8,128)(2,1)} %param.19, bf16[16,128,512]{2,1,0:T(8,128)(2,1)S(1)} %gather_fusion.1, pred[16]{0:T(512)(128)(4,1)S(1)} %and_bitcast_fusion, bf16[128,512]{1,0:T(8,128)(2,1)} %reduce-scatter.3.cloned.1.call-done), kind=kOutput, calls=%fused_computation.57 | convolution fusion | flops 1074987008 | bytes 10747920 | tf_op jit(solution)/shard_map/cikq,ikpq->cip/dot_general | solution.py:43
  146.8 0.9 convolution_convert_fusion.1
  147.9 20.2 %all-gather.11.cloned.1.call-done = bf16[128,4096]{0,1:T(8,128)(2,1)} async-done(((bf16[128,512]{0,1:T(8,128)(2,1)}), bf16[128,4096]{0,1:T(8,128)(2,1)}) %all-gather.11.cloned.1.call-update) | async-done | bytes 1048592 | tf_op jit(solution)/shard_map/all_gather | solution.py:34
  168.1 3.9 %gather_fusion.2 = bf16[24,128,512]{1,2,0:T(8,128)(2,1)} fusion(bf16[128,8,512]{0,2,1:T(8,128)(2,1)} %bitcast.182, s32[1024]{0:T(1024)S(1)} %pad_clamp_fusion.1), kind=kCustom, calls=%fused_computation.2.clone | custom fusion | bytes 6291552 | tf_op jit(solution)/shard_map/jit(_take)/gather | solution.py:13
  172.0 6.7 %fusion.4 = (bf16[128,24,512]{2,0,1:T(8,128)(2,1)}, bf16[128,24,512]{2,0,1:T(8,128)(2,1)S(1)}) fusion(bf16[24,64,512]{2,1,0:T(8,128)(2,1)} %all-gather.9.cloned.1.call-done, bf16[24,64,512]{2,1,0:T(8,128)(2,1)} %all-gather.7.cloned.1.call-done, bf16[24,128,512]{1,2,0:T(8,128)(2,1)} %gather_fusion.2, pred[24]{0:T(512)(128)(4,1)S(1)} %compare_and_fusion, ...), kind=kOutput, calls=%fused_computation.10 | convolution fusion | flops 410910720 | bytes 12584472 | tf_op jit(solution)/shard_map/ctr,trp->ctp/dot_general | solution.py:20
  178.7 4.1 %fusion.10 = f32[8,128,512]{2,0,1:T(8,128)S(1)} fusion(bf16[128,24,512]{2,0,1:T(8,128)(2,1)} %get-tuple-element.15, s32[24]{0:T(128)S(1)} %get-tuple-element.14), kind=kOutput, calls=%fused_computation.18 | convolution fusion | flops 25166016 | bytes 5242976 | tf_op jit(solution)/shard_map/ctp,tb->cbp/dot_general | solution.py:28
  182.8 2.3 add_convert_fusion
  185.2 1.4 copy.57
  187.8 2.0 gather_fusion.3
  189.9 28.8 %reduce-scatter.5.cloned.1.call-done = bf16[128,512]{1,0:T(8,128)(2,1)} async-done(((bf16[128,4096]{1,0:T(8,128)(2,1)}), bf16[128,512]{1,0:T(8,128)(2,1)}) %reduce-scatter.5.cloned.1.call-update) | async-done | bytes 131088 | tf_op jit(solution)/shard_map/reduce_scatter | solution.py:39
  218.7 6.8 %fusion.88 = bf16[16,4,8,128]{3,2,1,0:T(8,128)(2,1)S(1)} fusion(bf16[1,16,512,512]{3,2,1,0:T(8,128)(2,1)} %param.19, bf16[16,128,512]{2,1,0:T(8,128)(2,1)} %gather_fusion.3, pred[16]{0:T(512)(128)(4,1)S(1)} %and_bitcast_fusion, bf16[128,512]{1,0:T(8,128)(2,1)} %reduce-scatter.5.cloned.1.call-done), kind=kOutput, calls=%fused_computation.56 | convolution fusion | flops 1074987008 | bytes 10747920 | tf_op jit(solution)/shard_map/cikq,ikpq->cip/dot_general | solution.py:43
  (40 shorter events, 7.5 us)
Async XLA Ops:
  7.2 139.6 %copy-start = (bf16[4,128,128]{2,1,0:T(8,128)(2,1)S(1)}, bf16[4,128,128]{2,1,0:T(8,128)(2,1)}, u32[]{:S(2)}) copy-start(bf16[4,128,128]{2,1,0:T(8,128)(2,1)} %param.21) | copy-start | bytes 393220
  7.2 27.8 %all-gather.5.cloned.1.call-start = ((), (), s32[]{:S(2)}) async-start(), calls=%async_computation.2 | async-start | bytes 1179648 | tf_op jit(solution)/shard_map/all_gather | solution.py:34
  8.9 54.5 %all-gather.7.cloned.1.call-start = ((), (), s32[]{:S(2)}) async-start(), calls=%async_computation.3 | async-start | bytes 2359296 | tf_op jit(solution)/shard_map/all_gather | solution.py:73
  9.7 82.5 %all-gather.9.cloned.1.call-start = ((), (), s32[]{:S(2)}) async-start(), calls=%async_computation.4 | async-start | bytes 2359296 | tf_op jit(solution)/shard_map/all_gather | solution.py:72
  10.4 130.1 %reduce-scatter.3.cloned.1.call-start = ((), (), s32[]{:S(2)}) async-start(), calls=%async_computation.5 | async-start | bytes 1179648 | tf_op jit(solution)/shard_map/reduce_scatter | solution.py:39
  100.0 4.3 %copy-start.2 = (bf16[128,24,512]{2,0,1:T(8,128)(2,1)S(1)}, bf16[128,24,512]{2,0,1:T(8,128)(2,1)}, u32[]{:S(2)}) copy-start(bf16[128,24,512]{2,0,1:T(8,128)(2,1)} %get-tuple-element.18) | copy-start | bytes 9437188
  106.5 1.5 copy-start.4
  107.9 60.2 %all-gather.11.cloned.1.call-start = ((), (), s32[]{:S(2)}) async-start(), calls=%async_computation.6 | async-start | bytes 1179648 | tf_op jit(solution)/shard_map/all_gather | solution.py:34
  147.7 71.0 %reduce-scatter.5.cloned.1.call-start = ((), (), s32[]{:S(2)}) async-start(), calls=%async_computation.7 | async-start | bytes 1179648 | tf_op jit(solution)/shard_map/reduce_scatter | solution.py:39
  185.1 1.4 copy-start.3
  185.1 2.2 copy-start.1
Sparse Core Ops, SparseCore 0:
  10.2 24.7 all-gather.4
  36.6 26.8 all-gather.6
  65.0 27.1 all-gather.8
  108.0 32.4 reduce-scatter.2
  147.8 20.2 all-gather.10
  186.7 31.9 reduce-scatter.4
where the time goes:
time: 234 us; the launch traced here: 233 us
  waiting for transfers between devices  150 us (64%)
  matrix products  41.5 us (18%)
  local copies, waits for them, and re-layouts  20.9 us (9%)
  between operations  14.9 us (6%)
  blocking collectives  5.19 us (2%)
    reduce_scatter x2, waiting for transfers between devices, apply_operator(): lax.psum_scatter(far_field.astype(jnp.bfloat16), ('tiles', 'sub'), scatte...  60.7 us
    all_gather x2, waiting for transfers between devices, apply_operator(): lax.all_gather(vector, ('tiles', 'sub'), axis=1, tiled=True)  35 us
    all_gather x1, waiting for transfers between devices, tile_apply(): lax.all_gather(basis_out, 'rhs', axis=0, tiled=True)  28.8 us
    all_gather x1, waiting for transfers between devices, tile_apply(): lax.all_gather(basis_in, 'rhs', axis=0, tiled=True)  24.4 us
    dot_general x2, matrix products, tile_terms(): jnp.einsum('ctr,trp->ctp', coefficients, basis_out, preferred_element_typ...  14.4 us
    dot_general x2, matrix products, apply_operator(): jnp.einsum('cikq,ikpq->cip', picked, near_blocks, preferred_element_type=...  13 us
    unnamed x22, local copies, waits for them, and re-layouts  9.77 us
    dot_general x2, matrix products, tile_terms(): jnp.einsum('ctp,tb->cbp', lower, onehot, preferred_element_type=jnp.float32)  8.39 us
  transfers between devices with their start and end apart: 6, of which 6 were waited for; matrix products, arithmetic and copies ran while one was open for 5% of the time, Pallas kernels for 0%

commit v1 on v0

--- a/solution.py
+++ b/solution.py
@@ -2,10 +2,35 @@
 import jax.numpy as jnp
 from jax import lax
 from jax.sharding import PartitionSpec as P
+from jax.lax import axis_index, axis_size, ppermute
 
 BLK = 512
 RMAX = 64
 JB = 128
+
+
+def change_groups(array_in, mesh_ax, along_dim):
+    latest, arr_now, left_arr = (axis_size(mesh_ax), axis_index(mesh_ax), array_in.shape[along_dim])
+    pool = tuple((rr * latest if nth == along_dim else rr for nth, rr in enumerate(array_in.shape)))
+    ready = lax.dynamic_update_slice_in_dim(
+        jnp.zeros(pool, array_in.dtype), array_in, arr_now * left_arr, axis=along_dim
+    )
+    local_next = inter = array_in
+    for num in range(1, latest // 2 + 1):
+        local_next = ppermute(
+            local_next, mesh_ax, tuple(((nth, (nth + 1) % latest) for nth in range(latest)))
+        )
+        ready = lax.dynamic_update_slice_in_dim(
+            ready, local_next, (arr_now - num) % latest * left_arr, axis=along_dim
+        )
+        if 2 * num < latest:
+            inter = ppermute(
+                inter, mesh_ax, tuple(((nth, (nth - 1) % latest) for nth in range(latest)))
+            )
+            ready = lax.dynamic_update_slice_in_dim(
+                ready, inter, (arr_now + num) % latest * left_arr, axis=along_dim
+            )
+    return ready
 
 
 def tile_terms(running, pieces, gathered):
@@ -31,9 +56,7 @@
 
 def apply_operator(vector, tile_apply, near_blocks, near_col):
     columns = vector.shape[0]
-    gathered = lax.all_gather(vector, ("tiles", "sub"), axis=1, tiled=True).reshape(
-        columns, -1, BLK
-    )
+    gathered = change_groups(vector, ("tiles", "sub"), along_dim=1).reshape(columns, -1, BLK)
     zero_sums = jnp.zeros(gathered.shape, jnp.float32)
     far_field = tile_apply(zero_sums, gathered).reshape(columns, -1)
     far_field = lax.psum_scatter(

time: 234 us -> 211 us (0.902)
  waiting for transfers between devices: 150 us -> 111 us
  starting transfers between devices: 0.42 us -> 22.9 us
  local copies, waits for them, and re-layouts: 20.9 us -> 17.2 us
    all_gather x2 -> x0, waiting for transfers between devices: 35 us -> none  [apply_operator(): lax.all_gather(vector, ('tiles', 'sub'), axis=1, tiled=True)]
    ppermute x0 -> x14, waiting for transfers between devices: none -> 26.5 us  [the longest x8 26.3 us: change_groups(): ppermute(local_next, mesh_ax, tuple(((nth, (nth + 1) % latest) for nth in...]
    all_gather x1, waiting for transfers between devices: 24.4 us -> 0.01 us  [tile_apply(): lax.all_gather(basis_in, 'rhs', axis=0, tiled=True)]
    ppermute x0 -> x14, starting transfers between devices: none -> 22.7 us  [the longest x6 22.1 us: change_groups(): ppermute(inter, mesh_ax, tuple(((nth, (nth - 1) % latest) for nth in rang...]
    all_gather x1, waiting for transfers between devices: 28.8 us -> 22.4 us  [tile_apply(): lax.all_gather(basis_out, 'rhs', axis=0, tiled=True)]
  transfers between devices with their start and end apart: 6 -> 18, of which waited for: 6 -> 11; matrix products, arithmetic and copies ran while one was open for 5% -> 5% of each run, Pallas kernels for 0% -> 0%
where the time goes in v1:
time: 211 us
  waiting for transfers between devices  111 us (53%)
  matrix products  41 us (19%)
  starting transfers between devices  22.9 us (11%)
  local copies, waits for them, and re-layouts  17.2 us (8%)
  between operations  14.9 us (7%)
  blocking collectives  4.25 us (2%)
    reduce_scatter x2, waiting for transfers between devices, apply_operator(): lax.psum_scatter(far_field.astype(jnp.bfloat16), ('tiles', 'sub'), scatte...  60.9 us
    ppermute x8, waiting for transfers between devices, change_groups(): ppermute(local_next, mesh_ax, tuple(((nth, (nth + 1) % latest) for nth in...  26.3 us
    all_gather x1, waiting for transfers between devices, tile_apply(): lax.all_gather(basis_out, 'rhs', axis=0, tiled=True)  22.4 us
    ppermute x6, starting transfers between devices, change_groups(): ppermute(inter, mesh_ax, tuple(((nth, (nth - 1) % latest) for nth in rang...  22.1 us
    dot_general x2, matrix products, tile_terms(): jnp.einsum('ctr,trp->ctp', coefficients, basis_out, preferred_element_typ...  15 us
    dot_general x2, matrix products, apply_operator(): jnp.einsum('cikq,ikpq->cip', picked, near_blocks, preferred_element_type=...  12.4 us
    unnamed x22, local copies, waits for them, and re-layouts  9.16 us
    dot_general x2, matrix products, tile_terms(): jnp.einsum('ctp,tb->cbp', lower, onehot, preferred_element_type=jnp.float32)  8.54 us
  transfers between devices with their start and end apart: 18, of which 11 were waited for; matrix products, arithmetic and copies ran while one was open for 5% of the time, Pallas kernels for 0%

profile of v1, /device:TPU:0, one launch (start us, length us, event | category | flops | bytes accessed | tf_op | source)
XLA Modules:
  0.0 210.8 jit_solution(211242523118072559)
XLA Ops:
  9.5 4.1 %collective-permute-start.1 = (bf16[128,512]{0,1:T(8,128)(2,1)S(1)}, bf16[128,512]{0,1:T(8,128)(2,1)S(1)}, u32[]{:S(2)}, u32[]{:S(2)}) collective-permute-start(bf16[128,512]{0,1:T(8,128)(2,1)S(1)} %copy.58), channel_id=1, source_target_pairs={{0,13},{1,0},{4,1},{5,4},{8,5},{9,8},{12,9},{13,12},{2,15},{3,2},{... | collective-permute-start | bytes 393224 | tf_op jit(solution)/shard_map/ppermute | solution.py:27
  18.1 4.3 %all-reduce.3 = (s32[24]{0:T(128)S(1)}, s32[24]{0:T(128)S(1)}, s32[24]{0:T(128)S(1)}) all-reduce(s32[24]{0:T(128)S(1)} %dynamic-update-slice.2, s32[24]{0:T(128)S(1)} %dynamic-update-slice.1, s32[24]{0:T(128)S(1)} %dynamic-update-slice), channel_id=1, replica_groups=mesh['groups'=2,'tiles'=4,'rhs'=2,'sub'=2] {'rhs'}, use_global_device_ids=true, to_apply=%add.2 | all-reduce | flops 72 | bytes 576
  22.9 3.5 %collective-permute-start.3 = (bf16[128,512]{0,1:T(8,128)(2,1)S(1)}, bf16[128,512]{0,1:T(8,128)(2,1)S(1)}, u32[]{:S(2)}, u32[]{:S(2)}) collective-permute-start(bf16[128,512]{0,1:T(8,128)(2,1)S(1)} %collective-permute-done.1), channel_id=1, source_target_pairs={{0,13},{1,0},{4,1},{5,4},{8,5},{9,8},{12,9},{13,12},{2,15},{3,2},{... | collective-permute-start | bytes 393224 | tf_op jit(solution)/shard_map/ppermute | solution.py:27
  26.5 3.3 %collective-permute-done.2 = bf16[128,512]{0,1:T(8,128)(2,1)S(1)} collective-permute-done((bf16[128,512]{0,1:T(8,128)(2,1)S(1)}, bf16[128,512]{0,1:T(8,128)(2,1)S(1)}, u32[]{:S(2)}, u32[]{:S(2)}) %collective-permute-start.2) | collective-permute-done | bytes 131104 | tf_op jit(solution)/shard_map/ppermute | solution.py:20
  29.9 3.7 %collective-permute-start.5 = (bf16[128,512]{0,1:T(8,128)(2,1)S(1)}, bf16[128,512]{0,1:T(8,128)(2,1)S(1)}, u32[]{:S(2)}, u32[]{:S(2)}) collective-permute-start(bf16[128,512]{0,1:T(8,128)(2,1)S(1)} %collective-permute-done.3), channel_id=1, source_target_pairs={{0,13},{1,0},{4,1},{5,4},{8,5},{9,8},{12,9},{13,12},{2,15},{3,2},{... | collective-permute-start | bytes 393224 | tf_op jit(solution)/shard_map/ppermute | solution.py:27
  33.7 3.0 %collective-permute-done.4 = bf16[128,512]{0,1:T(8,128)(2,1)S(1)} collective-permute-done((bf16[128,512]{0,1:T(8,128)(2,1)S(1)}, bf16[128,512]{0,1:T(8,128)(2,1)S(1)}, u32[]{:S(2)}, u32[]{:S(2)}) %collective-permute-start.4) | collective-permute-done | bytes 131104 | tf_op jit(solution)/shard_map/ppermute | solution.py:20
  36.7 6.1 %collective-permute-done.6 = bf16[128,512]{0,1:T(8,128)(2,1)S(1)} collective-permute-done((bf16[128,512]{0,1:T(8,128)(2,1)S(1)}, bf16[128,512]{0,1:T(8,128)(2,1)S(1)}, u32[]{:S(2)}, u32[]{:S(2)}) %collective-permute-start.6) | collective-permute-done | bytes 131104 | tf_op jit(solution)/shard_map/ppermute | solution.py:20
  43.4 2.5 %gather_fusion = bf16[24,128,512]{2,1,0:T(8,128)(2,1)} fusion(bf16[128,8,512]{2,0,1:T(8,128)(2,1)S(1)} %copy.61, s32[1024]{0:T(1024)S(1)} %pad_clamp_fusion.1), kind=kCustom, calls=%fused_computation.clone | custom fusion | bytes 6291552 | tf_op jit(solution)/shard_map/jit(_take)/gather | solution.py:38
  45.9 22.4 %all-gather.5.cloned.1.call-done = bf16[24,64,512]{2,1,0:T(8,128)(2,1)} async-done(((bf16[12,64,512]{2,1,0:T(8,128)(2,1)}), bf16[24,64,512]{2,1,0:T(8,128)(2,1)}) %all-gather.5.cloned.1.call-update) | async-done | bytes 1572880 | tf_op jit(solution)/shard_map/all_gather | solution.py:95
  68.3 7.8 %fusion.5 = (bf16[128,24,512]{2,0,1:T(8,128)(2,1)}, bf16[128,24,512]{2,0,1:T(8,128)(2,1)}) fusion(bf16[24,64,512]{2,1,0:T(8,128)(2,1)} %all-gather.5.cloned.1.call-done, bf16[24,64,512]{2,1,0:T(8,128)(2,1)} %all-gather.3.cloned.1.call-done, bf16[24,128,512]{2,1,0:T(8,128)(2,1)} %gather_fusion, pred[24]{0:T(512)(128)(4,1)S(1)} %compare_and_fusion, ...), kind=kOutput, calls=%fused_computation.13 | convolution fusion | flops 410910720 | bytes 12584472 | tf_op jit(solution)/shard_map/ctr,trp->ctp/dot_general | solution.py:45
  76.0 4.3 %fusion.14 = f32[8,128,512]{2,0,1:T(8,128)S(1)} fusion(bf16[128,24,512]{2,0,1:T(8,128)(2,1)} %get-tuple-element.17, s32[24]{0:T(128)S(1)} %get-tuple-element.14), kind=kOutput, calls=%fused_computation.22 | convolution fusion | flops 25166016 | bytes 5242976 | tf_op jit(solution)/shard_map/ctp,tb->cbp/dot_general | solution.py:53
  84.8 31.9 %reduce-scatter.3.cloned.1.call-done = bf16[128,512]{1,0:T(8,128)(2,1)} async-done(((bf16[128,4096]{1,0:T(8,128)(2,1)}), bf16[128,512]{1,0:T(8,128)(2,1)}) %reduce-scatter.3.cloned.1.call-update) | async-done | bytes 131088 | tf_op jit(solution)/shard_map/reduce_scatter | solution.py:62
  116.7 6.2 %fusion.93 = bf16[16,4,8,128]{3,2,1,0:T(8,128)(2,1)S(1)} fusion(bf16[1,16,512,512]{3,2,1,0:T(8,128)(2,1)} %param.19, bf16[16,128,512]{2,1,0:T(8,128)(2,1)S(1)} %gather_fusion.1, pred[16]{0:T(512)(128)(4,1)S(1)} %and_bitcast_fusion, bf16[128,512]{1,0:T(8,128)(2,1)} %reduce-scatter.3.cloned.1.call-done), kind=kOutput, calls=%fused_computation.57 | convolution fusion | flops 1074987008 | bytes 10747920 | tf_op jit(solution)/shard_map/cikq,ikpq->cip/dot_general | solution.py:66
  123.2 3.5 %collective-permute-start.8 = (bf16[128,512]{0,1:T(8,128)(2,1)S(1)}, bf16[128,512]{0,1:T(8,128)(2,1)S(1)}, u32[]{:S(2)}, u32[]{:S(2)}) collective-permute-start(bf16[128,512]{0,1:T(8,128)(2,1)S(1)} %bitcast.189), channel_id=1, source_target_pairs={{0,13},{1,0},{4,1},{5,4},{8,5},{9,8},{12,9},{13,12},{2,15},{3,2},{... | collective-permute-start | bytes 393224 | tf_op jit(solution)/shard_map/ppermute | solution.py:27
  126.9 2.7 %collective-permute-done.7 = bf16[128,512]{0,1:T(8,128)(2,1)S(1)} collective-permute-done((bf16[128,512]{0,1:T(8,128)(2,1)S(1)}, bf16[128,512]{0,1:T(8,128)(2,1)S(1)}, u32[]{:S(2)}, u32[]{:S(2)}) %collective-permute-start.7) | collective-permute-done | bytes 131104 | tf_op jit(solution)/shard_map/ppermute | solution.py:20
  129.6 3.6 %collective-permute-start.10 = (bf16[128,512]{0,1:T(8,128)(2,1)S(1)}, bf16[128,512]{0,1:T(8,128)(2,1)S(1)}, u32[]{:S(2)}, u32[]{:S(2)}) collective-permute-start(bf16[128,512]{0,1:T(8,128)(2,1)S(1)} %collective-permute-done.8), channel_id=1, source_target_pairs={{0,13},{1,0},{4,1},{5,4},{8,5},{9,8},{12,9},{13,12},{2,15},{3,2},{... | collective-permute-start | bytes 393224 | tf_op jit(solution)/shard_map/ppermute | solution.py:27
  133.2 2.7 %collective-permute-done.9 = bf16[128,512]{0,1:T(8,128)(2,1)S(1)} collective-permute-done((bf16[128,512]{0,1:T(8,128)(2,1)S(1)}, bf16[128,512]{0,1:T(8,128)(2,1)S(1)}, u32[]{:S(2)}, u32[]{:S(2)}) %collective-permute-start.9) | collective-permute-done | bytes 131104 | tf_op jit(solution)/shard_map/ppermute | solution.py:20
  135.9 3.6 %collective-permute-start.12 = (bf16[128,512]{0,1:T(8,128)(2,1)S(1)}, bf16[128,512]{0,1:T(8,128)(2,1)S(1)}, u32[]{:S(2)}, u32[]{:S(2)}) collective-permute-start(bf16[128,512]{0,1:T(8,128)(2,1)S(1)} %collective-permute-done.10), channel_id=1, source_target_pairs={{0,13},{1,0},{4,1},{5,4},{8,5},{9,8},{12,9},{13,12},{2,15},{3,2},{... | collective-permute-start | bytes 393224 | tf_op jit(solution)/shard_map/ppermute | solution.py:27
  139.6 2.5 %collective-permute-done.11 = bf16[128,512]{0,1:T(8,128)(2,1)S(1)} collective-permute-done((bf16[128,512]{0,1:T(8,128)(2,1)S(1)}, bf16[128,512]{0,1:T(8,128)(2,1)S(1)}, u32[]{:S(2)}, u32[]{:S(2)}) %collective-permute-start.11) | collective-permute-done | bytes 131104 | tf_op jit(solution)/shard_map/ppermute | solution.py:20
  142.1 6.1 %collective-permute-done.13 = bf16[128,512]{0,1:T(8,128)(2,1)S(1)} collective-permute-done((bf16[128,512]{0,1:T(8,128)(2,1)S(1)}, bf16[128,512]{0,1:T(8,128)(2,1)S(1)}, u32[]{:S(2)}, u32[]{:S(2)}) %collective-permute-start.13) | collective-permute-done | bytes 131104 | tf_op jit(solution)/shard_map/ppermute | solution.py:20
  151.3 7.3 %fusion.4 = (bf16[128,24,512]{2,0,1:T(8,128)(2,1)}, bf16[128,24,512]{2,0,1:T(8,128)(2,1)}) fusion(bf16[24,64,512]{2,1,0:T(8,128)(2,1)} %all-gather.5.cloned.1.call-done, bf16[24,64,512]{2,1,0:T(8,128)(2,1)S(1)} %copy-done.3, bf16[24,128,512]{2,1,0:T(8,128)(2,1)} %gather_fusion.2, pred[24]{0:T(512)(128)(4,1)S(1)} %compare_and_fusion, ...), kind=kOutput, calls=%fused_computation.10 | convolution fusion | flops 410910720 | bytes 12584472 | tf_op jit(solution)/shard_map/ctr,trp->ctp/dot_general | solution.py:45
  158.6 4.3 %fusion.10 = f32[8,128,512]{2,0,1:T(8,128)S(1)} fusion(bf16[128,24,512]{2,0,1:T(8,128)(2,1)} %get-tuple-element.15, s32[24]{0:T(128)S(1)} %get-tuple-element.14), kind=kOutput, calls=%fused_computation.18 | convolution fusion | flops 25166016 | bytes 5242976 | tf_op jit(solution)/shard_map/ctp,tb->cbp/dot_general | solution.py:53
  168.0 29.1 %reduce-scatter.5.cloned.1.call-done = bf16[128,512]{1,0:T(8,128)(2,1)} async-done(((bf16[128,4096]{1,0:T(8,128)(2,1)}), bf16[128,512]{1,0:T(8,128)(2,1)}) %reduce-scatter.5.cloned.1.call-update) | async-done | bytes 131088 | tf_op jit(solution)/shard_map/reduce_scatter | solution.py:62
  197.1 6.2 %fusion.88 = bf16[16,4,8,128]{3,2,1,0:T(8,128)(2,1)S(1)} fusion(bf16[1,16,512,512]{3,2,1,0:T(8,128)(2,1)} %param.19, bf16[16,128,512]{2,1,0:T(8,128)(2,1)S(1)} %gather_fusion.3, pred[16]{0:T(512)(128)(4,1)S(1)} %and_bitcast_fusion, bf16[128,512]{1,0:T(8,128)(2,1)} %reduce-scatter.5.cloned.1.call-done), kind=kOutput, calls=%fused_computation.56 | convolution fusion | flops 1074987008 | bytes 10747920 | tf_op jit(solution)/shard_map/cikq,ikpq->cip/dot_general | solution.py:66
  (80 shorter events, 21.4 us)
Async XLA Ops:
  7.2 115.7 %copy-start = (bf16[4,128,128]{2,1,0:T(8,128)(2,1)S(1)}, bf16[4,128,128]{2,1,0:T(8,128)(2,1)}, u32[]{:S(2)}) copy-start(bf16[4,128,128]{2,1,0:T(8,128)(2,1)} %param.21) | copy-start | bytes 393220
  7.2 38.7 %all-gather.3.cloned.1.call-start = ((), (), s32[]{:S(2)}) async-start(), calls=%async_computation.2 | async-start | bytes 2359296 | tf_op jit(solution)/shard_map/all_gather | solution.py:96
  7.9 60.4 %all-gather.5.cloned.1.call-start = ((), (), s32[]{:S(2)}) async-start(), calls=%async_computation.3 | async-start | bytes 2359296 | tf_op jit(solution)/shard_map/all_gather | solution.py:95
  9.0 13.8 %collective-permute-start = (bf16[128,512]{0,1:T(8,128)(2,1)S(1)}, bf16[128,512]{0,1:T(8,128)(2,1)S(1)}, u32[]{:S(2)}, u32[]{:S(2)}) collective-permute-start(bf16[128,512]{0,1:T(8,128)(2,1)S(1)} %copy.58), channel_id=1, source_target_pairs={{0,1},{1,4},{4,5},{5,8},{8,9},{9,12},{12,13},{13,0},{2,3},{3,6},{6... | collective-permute-start | bytes 393224 | tf_op jit(solution)/shard_map/ppermute | solution.py:20
  9.5 13.4 %collective-permute-start.1 = (bf16[128,512]{0,1:T(8,128)(2,1)S(1)}, bf16[128,512]{0,1:T(8,128)(2,1)S(1)}, u32[]{:S(2)}, u32[]{:S(2)}) collective-permute-start(bf16[128,512]{0,1:T(8,128)(2,1)S(1)} %copy.58), channel_id=1, source_target_pairs={{0,13},{1,0},{4,1},{5,4},{8,5},{9,8},{12,9},{13,12},{2,15},{3,2},{... | collective-permute-start | bytes 393224 | tf_op jit(solution)/shard_map/ppermute | solution.py:27
  13.6 103.1 %reduce-scatter.3.cloned.1.call-start = ((), (), s32[]{:S(2)}) async-start(), calls=%async_computation.4 | async-start | bytes 1179648 | tf_op jit(solution)/shard_map/reduce_scatter | solution.py:62
  22.8 7.0 %collective-permute-start.2 = (bf16[128,512]{0,1:T(8,128)(2,1)S(1)}, bf16[128,512]{0,1:T(8,128)(2,1)S(1)}, u32[]{:S(2)}, u32[]{:S(2)}) collective-permute-start(bf16[128,512]{0,1:T(8,128)(2,1)S(1)} %collective-permute-done), channel_id=1, source_target_pairs={{0,1},{1,4},{4,5},{5,8},{8,9},{9,12},{12,13},{13,0},{2,3},{3,6},{6... | collective-permute-start | bytes 393224 | tf_op jit(solution)/shard_map/ppermute | solution.py:20
  22.9 7.0 %collective-permute-start.3 = (bf16[128,512]{0,1:T(8,128)(2,1)S(1)}, bf16[128,512]{0,1:T(8,128)(2,1)S(1)}, u32[]{:S(2)}, u32[]{:S(2)}) collective-permute-start(bf16[128,512]{0,1:T(8,128)(2,1)S(1)} %collective-permute-done.1), channel_id=1, source_target_pairs={{0,13},{1,0},{4,1},{5,4},{8,5},{9,8},{12,9},{13,12},{2,15},{3,2},{... | collective-permute-start | bytes 393224 | tf_op jit(solution)/shard_map/ppermute | solution.py:27
  29.8 6.9 %collective-permute-start.4 = (bf16[128,512]{0,1:T(8,128)(2,1)S(1)}, bf16[128,512]{0,1:T(8,128)(2,1)S(1)}, u32[]{:S(2)}, u32[]{:S(2)}) collective-permute-start(bf16[128,512]{0,1:T(8,128)(2,1)S(1)} %collective-permute-done.2), channel_id=1, source_target_pairs={{0,1},{1,4},{4,5},{5,8},{8,9},{9,12},{12,13},{13,0},{2,3},{3,6},{6... | collective-permute-start | bytes 393224 | tf_op jit(solution)/shard_map/ppermute | solution.py:20
  29.9 6.8 %collective-permute-start.5 = (bf16[128,512]{0,1:T(8,128)(2,1)S(1)}, bf16[128,512]{0,1:T(8,128)(2,1)S(1)}, u32[]{:S(2)}, u32[]{:S(2)}) collective-permute-start(bf16[128,512]{0,1:T(8,128)(2,1)S(1)} %collective-permute-done.3), channel_id=1, source_target_pairs={{0,13},{1,0},{4,1},{5,4},{8,5},{9,8},{12,9},{13,12},{2,15},{3,2},{... | collective-permute-start | bytes 393224 | tf_op jit(solution)/shard_map/ppermute | solution.py:27
  36.6 6.2 %collective-permute-start.6 = (bf16[128,512]{0,1:T(8,128)(2,1)S(1)}, bf16[128,512]{0,1:T(8,128)(2,1)S(1)}, u32[]{:S(2)}, u32[]{:S(2)}) collective-permute-start(bf16[128,512]{0,1:T(8,128)(2,1)S(1)} %collective-permute-done.4), channel_id=1, source_target_pairs={{0,1},{1,4},{4,5},{5,8},{8,9},{9,12},{12,13},{13,0},{2,3},{3,6},{6... | collective-permute-start | bytes 393224 | tf_op jit(solution)/shard_map/ppermute | solution.py:20
  76.0 4.3 %copy-start.2 = (bf16[128,24,512]{2,0,1:T(8,128)(2,1)S(1)}, bf16[128,24,512]{2,0,1:T(8,128)(2,1)}, u32[]{:S(2)}) copy-start(bf16[128,24,512]{2,0,1:T(8,128)(2,1)} %get-tuple-element.18) | copy-start | bytes 9437188
  82.6 1.5 copy-start.4
  84.0 113.1 %reduce-scatter.5.cloned.1.call-start = ((), (), s32[]{:S(2)}) async-start(), calls=%async_computation.5 | async-start | bytes 1179648 | tf_op jit(solution)/shard_map/reduce_scatter | solution.py:62
  123.1 6.4 %collective-permute-start.7 = (bf16[128,512]{0,1:T(8,128)(2,1)S(1)}, bf16[128,512]{0,1:T(8,128)(2,1)S(1)}, u32[]{:S(2)}, u32[]{:S(2)}) collective-permute-start(bf16[128,512]{0,1:T(8,128)(2,1)S(1)} %bitcast.188), channel_id=1, source_target_pairs={{0,1},{1,4},{4,5},{5,8},{8,9},{9,12},{12,13},{13,0},{2,3},{3,6},{6... | collective-permute-start | bytes 393224 | tf_op jit(solution)/shard_map/ppermute | solution.py:20
  123.2 6.4 %collective-permute-start.8 = (bf16[128,512]{0,1:T(8,128)(2,1)S(1)}, bf16[128,512]{0,1:T(8,128)(2,1)S(1)}, u32[]{:S(2)}, u32[]{:S(2)}) collective-permute-start(bf16[128,512]{0,1:T(8,128)(2,1)S(1)} %bitcast.189), channel_id=1, source_target_pairs={{0,13},{1,0},{4,1},{5,4},{8,5},{9,8},{12,9},{13,12},{2,15},{3,2},{... | collective-permute-start | bytes 393224 | tf_op jit(solution)/shard_map/ppermute | solution.py:27
  129.6 6.3 %collective-permute-start.9 = (bf16[128,512]{0,1:T(8,128)(2,1)S(1)}, bf16[128,512]{0,1:T(8,128)(2,1)S(1)}, u32[]{:S(2)}, u32[]{:S(2)}) collective-permute-start(bf16[128,512]{0,1:T(8,128)(2,1)S(1)} %collective-permute-done.7), channel_id=1, source_target_pairs={{0,1},{1,4},{4,5},{5,8},{8,9},{9,12},{12,13},{13,0},{2,3},{3,6},{6... | collective-permute-start | bytes 393224 | tf_op jit(solution)/shard_map/ppermute | solution.py:20
  129.6 6.3 %collective-permute-start.10 = (bf16[128,512]{0,1:T(8,128)(2,1)S(1)}, bf16[128,512]{0,1:T(8,128)(2,1)S(1)}, u32[]{:S(2)}, u32[]{:S(2)}) collective-permute-start(bf16[128,512]{0,1:T(8,128)(2,1)S(1)} %collective-permute-done.8), channel_id=1, source_target_pairs={{0,13},{1,0},{4,1},{5,4},{8,5},{9,8},{12,9},{13,12},{2,15},{3,2},{... | collective-permute-start | bytes 393224 | tf_op jit(solution)/shard_map/ppermute | solution.py:27
  135.9 6.2 %collective-permute-start.11 = (bf16[128,512]{0,1:T(8,128)(2,1)S(1)}, bf16[128,512]{0,1:T(8,128)(2,1)S(1)}, u32[]{:S(2)}, u32[]{:S(2)}) collective-permute-start(bf16[128,512]{0,1:T(8,128)(2,1)S(1)} %collective-permute-done.9), channel_id=1, source_target_pairs={{0,1},{1,4},{4,5},{5,8},{8,9},{9,12},{12,13},{13,0},{2,3},{3,6},{6... | collective-permute-start | bytes 393224 | tf_op jit(solution)/shard_map/ppermute | solution.py:20
  135.9 6.2 %collective-permute-start.12 = (bf16[128,512]{0,1:T(8,128)(2,1)S(1)}, bf16[128,512]{0,1:T(8,128)(2,1)S(1)}, u32[]{:S(2)}, u32[]{:S(2)}) collective-permute-start(bf16[128,512]{0,1:T(8,128)(2,1)S(1)} %collective-permute-done.10), channel_id=1, source_target_pairs={{0,13},{1,0},{4,1},{5,4},{8,5},{9,8},{12,9},{13,12},{2,15},{3,2},{... | collective-permute-start | bytes 393224 | tf_op jit(solution)/shard_map/ppermute | solution.py:27
  142.1 6.2 %collective-permute-start.13 = (bf16[128,512]{0,1:T(8,128)(2,1)S(1)}, bf16[128,512]{0,1:T(8,128)(2,1)S(1)}, u32[]{:S(2)}, u32[]{:S(2)}) collective-permute-start(bf16[128,512]{0,1:T(8,128)(2,1)S(1)} %collective-permute-done.11), channel_id=1, source_target_pairs={{0,1},{1,4},{4,5},{5,8},{8,9},{9,12},{12,13},{13,0},{2,3},{3,6},{6... | collective-permute-start | bytes 393224 | tf_op jit(solution)/shard_map/ppermute | solution.py:20
  148.8 2.5 %copy-start.3 = (bf16[24,64,512]{2,1,0:T(8,128)(2,1)S(1)}, bf16[24,64,512]{2,1,0:T(8,128)(2,1)}, u32[]{:S(2)}) copy-start(bf16[24,64,512]{2,1,0:T(8,128)(2,1)} %all-gather.3.cloned.1.call-done) | copy-start | bytes 4718596
  158.6 4.3 %copy-start.1 = (bf16[128,24,512]{2,0,1:T(8,128)(2,1)S(1)}, bf16[128,24,512]{2,0,1:T(8,128)(2,1)}, u32[]{:S(2)}) copy-start(bf16[128,24,512]{2,0,1:T(8,128)(2,1)} %get-tuple-element.16) | copy-start | bytes 9437188
Sparse Core Ops, SparseCore 0:
  9.6 29.8 all-gather.2
  41.0 27.1 all-gather.4
  84.1 32.4 reduce-scatter.2
  166.7 30.3 reduce-scatter.4
